TPU v7x, 32 devices: a whole 2x2x4 slice. The times are simulated.
32 devices in a mesh: fsdp: 16 (over z, y, x), dp: 2 (over core).
Axes of the slice: x: 2, y: 2, z: 4, core: 2. Of those that a mesh axis runs over, the one named last changes fastest.
Arguments:
- grad_parts: bfloat16 [2, 16, 512, 512], P('dp', None, 'fsdp'), may hold values from -2.5 to 2.5
- weights: float32 [16, 512, 512], P(None, 'fsdp', 'dp'), may hold values from -6 to 6
- left_stat: float32 [48, 512, 512], P('fsdp', 'dp'), may hold values from -6 to 6
- right_stat: float32 [48, 512, 512], P('fsdp', 'dp'), may hold values from -6 to 6
- left_codes: bfloat16 [48, 512, 512], P('fsdp'), may hold values from -1 to 1
- right_codes: bfloat16 [48, 512, 512], P('fsdp', 'dp'), may hold values from -1 to 1
- left_scales: float32 [48, 512], P('fsdp'), may hold values from 0.3 to 3
- right_scales: float32 [48, 512], P('fsdp', 'dp'), may hold values from 0.1 to 27
- owners: int32 [16], replicated, may hold values from 0 to 15, as said below
Outputs:
- new_weights: float32 [16, 512, 512], P(None, 'fsdp', 'dp')
- new_left_stat: float32 [48, 512, 512], P('fsdp', 'dp')
- new_right_stat: float32 [48, 512, 512], P('fsdp', 'dp')
Inputs may be any that keep to these rules, and one draw needn't show every extreme that they name: `owners`: each owner is named by at most 3 blocks, and some owner by exactly 3 blocks.
All inputs are finite; a program needn't handle non-finite values.
Results may differ from a plain program's by a relative error of at most 0.0095.
Values may be sent and summed in bfloat16 or wider, within the bound.
A program may use at most 64 MiB of HBM per device.

v0:
```python
import jax
import jax.numpy as jnp
from jax import lax
from jax.sharding import PartitionSpec as P

stat_decay = 0.95
step_size = 0.5
epsilon = 1e-06


def slot_table(owners, capacity):
    count = owners.shape[0]
    index = jnp.arange(count, dtype=jnp.int32)
    earlier = (owners[:, None] == owners[None, :]) & (index[None, :] < index[:, None])
    rank = jnp.sum(earlier.astype(jnp.int32), axis=1)
    return owners * capacity + rank


def route_rows(summed, picker, owner_count, capacity):
    blocks = summed.shape[0]
    flat = summed.reshape(blocks, -1)
    placed = jnp.einsum("bj,bx->jx", picker, flat, preferred_element_type=jnp.float32).astype(
        jnp.bfloat16
    )
    return placed.reshape(owner_count, capacity, summed.shape[1], summed.shape[2])


def local(
    grad_parts,
    weights,
    left_stat,
    right_stat,
    left_codes,
    right_codes,
    left_scales,
    right_scales,
    owners,
):
    owner_count = lax.axis_size("fsdp")
    replica = lax.axis_index("dp")
    capacity = left_stat.shape[0]
    piece_width = left_stat.shape[1]
    block_width = left_codes.shape[1]
    slot_of = slot_table(owners, capacity)
    slot_ids = jnp.arange(owner_count * capacity, dtype=jnp.int32)
    picker = (slot_of[:, None] == slot_ids[None, :]).astype(jnp.bfloat16)
    partial_value = grad_parts[0].astype(jnp.float32)
    summed = lax.psum_scatter(
        partial_value.astype(jnp.bfloat16), "dp", scatter_dimension=2, tiled=True
    )
    routed = route_rows(summed, picker, owner_count, capacity)
    arrived = lax.all_to_all(routed, "fsdp", split_axis=0, concat_axis=2, tiled=True)
    column_part = arrived.reshape(capacity, block_width, piece_width)
    whole_grad = lax.all_gather(column_part, "dp", axis=2, tiled=True)
    first_row = replica * piece_width
    rows_mine = lax.dynamic_slice_in_dim(whole_grad, first_row, piece_width, 1)
    cols_mine = lax.dynamic_slice_in_dim(whole_grad, first_row, piece_width, 2)
    gram_left = jnp.einsum(
        "srk,sck->src", rows_mine, whole_grad, preferred_element_type=jnp.float32
    )
    gram_right = jnp.einsum(
        "skr,skc->src", cols_mine, whole_grad, preferred_element_type=jnp.float32
    )
    left_new = stat_decay * left_stat + (1.0 - stat_decay) * gram_left
    right_new = stat_decay * right_stat + (1.0 - stat_decay) * gram_right
    left_factor = (left_codes.astype(jnp.float32) * left_scales[:, :, None]).astype(jnp.bfloat16)
    right_factor = (right_codes.astype(jnp.float32) * right_scales[:, :, None]).astype(jnp.bfloat16)
    mixed = jnp.einsum(
        "sik,sck->sic", whole_grad, right_factor, preferred_element_type=jnp.float32
    ).astype(jnp.bfloat16)
    precond = jnp.einsum("sik,skc->sic", left_factor, mixed, preferred_element_type=jnp.float32)
    part_squares = jnp.sum(precond * precond, axis=(1, 2))
    total_squares = lax.psum(part_squares, "dp")
    grad_squares = jnp.sum(jnp.square(whole_grad.astype(jnp.float32)), axis=(1, 2))
    graft_ratio = jnp.sqrt(grad_squares) * lax.rsqrt(total_squares + epsilon)
    update = step_size * graft_ratio[:, None, None] * precond
    returned = lax.all_to_all(update, "fsdp", split_axis=1, concat_axis=0, tiled=True)
    my_update = jnp.take(returned, slot_of, axis=0)
    new_weights = weights - my_update
    return (new_weights, left_new, right_new)


def solution(mesh):
    return jax.shard_map(
        local,
        mesh=mesh,
        in_specs=(
            P("dp", None, "fsdp", None),
            P(None, "fsdp", "dp"),
            P("fsdp", "dp", None),
            P("fsdp", "dp", None),
            P("fsdp", None, None),
            P("fsdp", "dp", None),
            P("fsdp", None),
            P("fsdp", "dp"),
            P(),
        ),
        out_specs=(P(None, "fsdp", "dp"), P("fsdp", "dp", None), P("fsdp", "dp", None)),
        check_vma=False,
    )
```

profile of v0, /device:TPU:16, one launch (start us, length us, event | category | flops | bytes accessed | tf_op | source)
XLA Modules:
  0.0 133.3 jit_solution(3694708061100863244)
XLA Ops:
  7.2 0.0 reduce-scatter.2.cloned.1.call-start
  7.2 0.7 reduce-scatter.2.cloned.1.call-update
  7.9 0.0 all-gather.2.cloned.1.call-start
  7.9 0.9 convert_reduce_fusion
  8.9 0.7 compare_and_fusion
  9.5 9.9 %reduce-scatter.2.cloned.1.call-done = bf16[16,32,256]{2,1,0:T(8,128)(2,1)} async-done(((bf16[16,32,512]{2,1,0:T(8,128)(2,1)}), bf16[16,32,256]{2,1,0:T(8,128)(2,1)}) %reduce-scatter.2.cloned.1.call-update) | async-done | bytes 262160 | tf_op jit(solution)/shard_map/reduce_scatter | solution.py:48
  19.5 1.1 copy.31
  20.6 0.5 convolution_convert_fusion
  21.0 0.2 copy.32
  21.2 25.9 %all_to_all.33 = bf16[16,3,32,256]{3,2,1,0:T(8,128)(2,1)S(1)} all-to-all(bf16[16,3,32,256]{3,2,1,0:T(8,128)(2,1)S(1)} %bitcast.20), channel_id=1, replica_groups=mesh['fsdp'=16,'dp'=2] {'fsdp'}, dimensions={0} | all-to-all | bytes 1572864 | tf_op jit(solution)/shard_map/all_to_all | solution.py:52
  47.2 0.0 copy-start.4
  47.2 0.0 copy-start.5
  47.2 0.9 copy.25
  48.1 0.0 all-gather.2.cloned.1.call-update
  48.1 9.8 %all-gather.2.cloned.1.call-done = bf16[3,512,512]{2,1,0:T(8,128)(2,1)} async-done(((bf16[3,512,256]{2,1,0:T(8,128)(2,1)}), bf16[3,512,512]{2,1,0:T(8,128)(2,1)}) %all-gather.2.cloned.1.call-update) | async-done | bytes 1572880 | tf_op jit(solution)/shard_map/all_gather | solution.py:54
  57.9 0.0 copy-done.4
  57.9 0.0 copy-done.5
  57.9 0.0 copy-start
  57.9 3.4 %multiply_reduce_fusion.1 = (f32[3]{0:T(128)S(1)}, f32[3,512,256]{2,1,0:T(8,128)S(1)}) fusion(bf16[3,512,512]{2,1,0:T(8,128)(2,1)} %all-gather.2.cloned.1.call-done, bf16[3,256,512]{2,1,0:T(8,128)(2,1)} %param.14, f32[3,256]{1,0:T(4,128)S(1)} %copy-done.5, bf16[3,512,512]{2,1,0:T(8,128)(2,1)} %param.13, f32[3,512]{1,0:T(4,128)S(1)} %copy-done.4), kind=kOutput, calls=%fused_computation.7 | convolution fusion | flops 810024960 | bytes 5514252 | tf_op jit(solution)/shard_map/sik,skc->sic/dot_general | solution.py:71
  61.4 2.4 %psum.7 = f32[3]{0:T(128)S(1)} all-reduce(f32[3]{0:T(128)S(1)} %get-tuple-element.5), channel_id=1, replica_groups=mesh['fsdp'=16,'dp'=2] {'dp'}, use_global_device_ids=true, to_apply=%region_4.0 | all-reduce | flops 3 | bytes 24 | tf_op jit(solution)/shard_map/psum | solution.py:73
  63.8 0.0 copy-done
  63.8 0.5 multiply_reduce_fusion
  64.3 0.2 broadcast_multiply_fusion
  64.6 2.4 %copy.26 = f32[3,512,256]{2,0,1:T(4,128)} copy(f32[3,512,256]{2,1,0:T(8,128)S(1)} %broadcast_multiply_fusion) | data formatting | bytes 3145728 | tf_op jit(solution)/shard_map/mul | solution.py:76
  66.9 0.0 copy-start.1
  66.9 7.1 %all-to-all-start.1 = ((f32[3,512,256]{2,0,1:T(4,128)}), f32[3,512,256]{2,0,1:T(4,128)}, u32[]{:S(2)}, u32[]{:S(2)}) async-start(f32[3,512,256]{2,0,1:T(4,128)} %copy.26), calls=%async_computation.2 | async-start | bytes 4194304 | tf_op jit(solution)/shard_map/all_to_all | solution.py:77
  74.0 0.0 copy-done.1
  74.0 0.0 copy-start.2
  74.1 1.8 %multiply_add_fusion = f32[3,256,512]{2,1,0:T(8,128)} fusion(f32[3,256,512]{2,1,0:T(8,128)S(1)} %copy-done.1, bf16[3,512,512]{2,1,0:T(8,128)(2,1)S(1)} %copy-done, s32[]{:T(128)S(6)} %select_n.15), kind=kOutput, calls=%fused_computation.5 | convolution fusion | flops 403832832 | bytes 5505028 | tf_op jit(solution)/shard_map/skr,skc->src/dot_general | solution.py:61
  75.9 0.0 copy-done.2
  75.9 1.8 %multiply_add_fusion.1 = f32[3,256,512]{2,1,0:T(8,128)} fusion(f32[3,256,512]{2,1,0:T(8,128)S(1)} %copy-done.2, bf16[3,512,512]{2,1,0:T(8,128)(2,1)S(1)} %copy-done, s32[]{:T(128)S(6)} %select_n.15), kind=kOutput, calls=%fused_computation.6 | convolution fusion | flops 403832832 | bytes 5505028 | tf_op jit(solution)/shard_map/srk,sck->src/dot_general | solution.py:58
  77.7 45.0 %all-to-all-done.1 = f32[3,512,256]{2,0,1:T(4,128)} async-done(((f32[3,512,256]{2,0,1:T(4,128)}), f32[3,512,256]{2,0,1:T(4,128)}, u32[]{:S(2)}, u32[]{:S(2)}) %all-to-all-start.1) | async-done | bytes 1572896 | tf_op jit(solution)/shard_map/all_to_all | solution.py:77
  122.6 1.9 %copy.27 = f32[3,512,256]{2,1,0:T(8,128)S(1)} copy(f32[3,512,256]{2,0,1:T(4,128)} %all-to-all-done.1) | data formatting | bytes 3145728 | tf_op jit(solution)/shard_map/all_to_all | solution.py:77
  124.5 0.0 copy-start.3
  124.5 0.1 copy.28
  124.6 0.6 gather_fusion
  125.2 0.3 copy-done.3
  125.6 0.9 select_subtract_fusion
  (3 shorter events, 0.0 us)
Async XLA Ops:
  7.2 12.3 %reduce-scatter.2.cloned.1.call-start = ((), (), s32[]{:S(2)}) async-start(), calls=%async_computation.3 | async-start | bytes 786432 | tf_op jit(solution)/shard_map/reduce_scatter | solution.py:48
  7.9 50.0 %all-gather.2.cloned.1.call-start = ((), (), s32[]{:S(2)}) async-start(), calls=%async_computation.4 | async-start | bytes 2359296 | tf_op jit(solution)/shard_map/all_gather | solution.py:54
  47.2 10.8 %copy-start.4 = (f32[3,512]{1,0:T(4,128)S(1)}, f32[3,512]{1,0:T(4,128)}, u32[]{:S(2)}) copy-start(f32[3,512]{1,0:T(4,128)} %param.15) | copy-start | bytes 18436
  47.2 10.8 %copy-start.5 = (f32[3,256]{1,0:T(4,128)S(1)}, f32[3,256]{1,0:T(4,128)}, u32[]{:S(2)}) copy-start(f32[3,256]{1,0:T(4,128)} %param.16) | copy-start | bytes 9220
  57.9 5.9 %copy-start = (bf16[3,512,512]{2,1,0:T(8,128)(2,1)S(1)}, bf16[3,512,512]{2,1,0:T(8,128)(2,1)}, u32[]{:S(2)}) copy-start(bf16[3,512,512]{2,1,0:T(8,128)(2,1)} %all-gather.2.cloned.1.call-done) | copy-start | bytes 4718596
  66.9 7.1 %copy-start.1 = (f32[3,256,512]{2,1,0:T(8,128)S(1)}, f32[3,256,512]{2,1,0:T(8,128)}, u32[]{:S(2)}) copy-start(f32[3,256,512]{2,1,0:T(8,128)} %param.12) | copy-start | bytes 4718596
  66.9 55.7 %all-to-all-start.1 = ((f32[3,512,256]{2,0,1:T(4,128)}), f32[3,512,256]{2,0,1:T(4,128)}, u32[]{:S(2)}, u32[]{:S(2)}) async-start(f32[3,512,256]{2,0,1:T(4,128)} %copy.26), calls=%async_computation.2 | async-start | bytes 4194304 | tf_op jit(solution)/shard_map/all_to_all | solution.py:77
  74.0 1.8 %copy-start.2 = (f32[3,256,512]{2,1,0:T(8,128)S(1)}, f32[3,256,512]{2,1,0:T(8,128)}, u32[]{:S(2)}) copy-start(f32[3,256,512]{2,1,0:T(8,128)} %param.11) | copy-start | bytes 4718596
  124.5 1.0 copy-start.3
Sparse Core Ops, SparseCore 0:
  10.2 9.2 reduce-scatter.1
  48.3 9.6 all-gather.1
where the time goes:
time: 134 us; the launch traced here: 133 us
  waiting for transfers between devices  65.4 us (49%)
  blocking collectives  28.4 us (21%)
  between operations  14.1 us (11%)
  local copies, waits for them, and re-layouts  7.53 us (6%)
  matrix products  7.48 us (6%)
  starting transfers between devices  7.16 us (5%)
  other arithmetic  3.23 us (2%)
    all_to_all x1, waiting for transfers between devices, local(): lax.all_to_all(update, 'fsdp', split_axis=1, concat_axis=0, tiled=True)  45 us
    all_to_all x1, blocking collectives, local(): lax.all_to_all(routed, 'fsdp', split_axis=0, concat_axis=2, tiled=True)  25.9 us
    reduce_scatter x1, waiting for transfers between devices, local(): lax.psum_scatter(partial_value.astype(jnp.bfloat16), 'dp', scatter_dimens...  9.93 us
    all_gather x1, waiting for transfers between devices, local(): whole_grad = lax.all_gather(column_part, 'dp', axis=2, tiled=True)  9.8 us
    all_to_all x1, starting transfers between devices, local(): lax.all_to_all(update, 'fsdp', split_axis=1, concat_axis=0, tiled=True)  7.08 us
    dot_general x1, matrix products, local(): jnp.einsum('sik,skc->sic', left_factor, mixed, preferred_element_type=jnp...  3.42 us
  transfers between devices with their start and end apart: 3, of which 3 were waited for; matrix products, arithmetic and copies ran while one was open for 4% of the time, Pallas kernels for 0%

commit v1 on v0

--- a/solution.py
+++ b/solution.py
@@ -1,11 +1,16 @@
+import functools
+
 import jax
 import jax.numpy as jnp
 from jax import lax
+from jax.experimental import pallas as pl
+from jax.experimental.pallas import tpu as pltpu
 from jax.sharding import PartitionSpec as P
 
 stat_decay = 0.95
 step_size = 0.5
 epsilon = 1e-06
+MESH = pl.DeviceIdType.MESH
 
 
 def slot_table(owners, capacity):
@@ -16,6 +21,246 @@
     return owners * capacity + rank
 
 
+def greet(n, me, core):
+    barrier = pltpu.get_barrier_semaphore()
+
+    @pl.loop(1, n)
+    def _(k):
+        peer = lax.rem(me + k, n)
+        pl.semaphore_signal(barrier, inc=1, device_id=(peer, core), device_id_type=MESH)
+
+    pl.semaphore_signal(barrier, inc=1, device_id=(me, 1 - core), device_id_type=MESH)
+    pl.semaphore_wait(barrier, n)
+
+
+def scatter_kernel(
+    n, cap, source_ref, grad_ref, whole, theirs, summed, stage,
+    swap_send, swap_recv, out_send, out_recv, fwd_send, fwd_recv, own_sem,
+):
+    me = lax.axis_index("fsdp")
+    core = lax.axis_index("dp")
+    blocks, rows, _ = grad_ref.shape
+    half = rows // 2
+    greet(n, me, core)
+
+    other_rows = pl.ds(pl.multiple_of((1 - core) * half, half), half)
+    my_rows = pl.ds(pl.multiple_of(core * half, half), half)
+    swap = pltpu.make_async_remote_copy(
+        src_ref=grad_ref.at[:, other_rows, :], dst_ref=theirs,
+        send_sem=swap_send, recv_sem=swap_recv,
+        device_id=(me, 1 - core), device_id_type=MESH,
+    )
+    swap.start()
+    swap.wait()
+    summed[...] = (
+        grad_ref[:, my_rows, :].astype(jnp.float32) + theirs[...].astype(jnp.float32)
+    ).astype(jnp.bfloat16)
+
+    @pl.loop(0, n * cap)
+    def _(j):
+        code = source_ref[j]
+        piece = summed[lax.max(code, 0)].astype(jnp.float32)
+        keep = jnp.where(code >= 0, 1.0, 0.0).astype(jnp.float32)
+        stage[j] = (piece * keep).astype(jnp.bfloat16)
+
+    def landing(device, its_core):
+        start = pl.multiple_of(device * rows + its_core * half, half)
+        return whole.at[:, pl.ds(start, half), :]
+
+    def outgoing(k):
+        peer = lax.rem(me + k, n)
+        return pltpu.make_async_remote_copy(
+            src_ref=stage.at[pl.ds(peer * cap, cap)], dst_ref=landing(me, core),
+            send_sem=out_send.at[k], recv_sem=out_recv.at[k],
+            device_id=(peer, core), device_id_type=MESH,
+        )
+
+    def incoming(k):
+        peer = lax.rem(me - k + n, n)
+        return pltpu.make_async_remote_copy(
+            src_ref=stage.at[pl.ds(peer * cap, cap)], dst_ref=landing(peer, core),
+            send_sem=out_send.at[k], recv_sem=out_recv.at[k],
+            device_id=(peer, core), device_id_type=MESH,
+        )
+
+    def forward(k, its_core):
+        peer = lax.rem(me - k + n, n)
+        return pltpu.make_async_remote_copy(
+            src_ref=landing(peer, its_core), dst_ref=landing(peer, its_core),
+            send_sem=fwd_send.at[k], recv_sem=fwd_recv.at[k],
+            device_id=(me, 1 - core), device_id_type=MESH,
+        )
+
+    @pl.loop(1, n)
+    def _(k):
+        outgoing(k).start()
+
+    own = pltpu.make_async_copy(stage.at[pl.ds(me * cap, cap)], landing(me, core), own_sem)
+    own.start()
+    own.wait()
+    forward(0, core).start()
+
+    @pl.loop(1, n)
+    def _(k):
+        incoming(k).wait_recv()
+        forward(k, core).start()
+
+    @pl.loop(1, n)
+    def _(k):
+        outgoing(k).wait_send()
+
+    @pl.loop(0, n)
+    def _(k):
+        forward(k, core).wait_send()
+        forward(k, 1 - core).wait_recv()
+
+
+def return_kernel(
+    n, cap, place_ref, scale_row_ref, pre_ref, squares_ref, weights_ref, out_ref,
+    landed, other_squares, graft, grafts,
+    swap_send, swap_recv, out_send, out_recv, tiny_send, tiny_recv,
+):
+    me = lax.axis_index("fsdp")
+    core = lax.axis_index("dp")
+    blocks, rows, _ = weights_ref.shape
+    greet(n, me, core)
+
+    def transfer(k, peer, source):
+        return pltpu.make_async_remote_copy(
+            src_ref=pre_ref.at[:, pl.ds(pl.multiple_of(peer * rows, rows), rows), :],
+            dst_ref=landed.at[pl.ds(source * cap, cap)],
+            send_sem=out_send.at[k], recv_sem=out_recv.at[k],
+            device_id=(peer, core), device_id_type=MESH,
+        )
+
+    def tiny(k, peer, source):
+        return pltpu.make_async_remote_copy(
+            src_ref=graft, dst_ref=grafts.at[source],
+            send_sem=tiny_send.at[k], recv_sem=tiny_recv.at[k],
+            device_id=(peer, core), device_id_type=MESH,
+        )
+
+    swap = pltpu.make_async_remote_copy(
+        src_ref=squares_ref, dst_ref=other_squares,
+        send_sem=swap_send, recv_sem=swap_recv,
+        device_id=(me, 1 - core), device_id_type=MESH,
+    )
+    swap.start()
+
+    @pl.loop(1, n)
+    def _(k):
+        transfer(k, lax.rem(me + k, n), me).start()
+
+    landed[pl.ds(me * cap, cap)] = pre_ref[
+        :, pl.ds(pl.multiple_of(me * rows, rows), rows), :
+    ]
+    swap.wait()
+    total = squares_ref[0] + other_squares[0]
+    scale = step_size * jnp.sqrt(squares_ref[1]) * lax.rsqrt(total + epsilon)
+    graft[...] = scale
+    grafts[me] = scale
+
+    @pl.loop(1, n)
+    def _(k):
+        tiny(k, lax.rem(me + k, n), me).start()
+
+    @pl.loop(1, n)
+    def _(k):
+        peer = lax.rem(me - k + n, n)
+        transfer(k, peer, peer).wait_recv()
+        tiny(k, peer, peer).wait_recv()
+
+    @pl.loop(0, blocks)
+    def _(b):
+        slot = place_ref[b]
+        factor = grafts[scale_row_ref[b]]
+        rank = lax.rem(slot, cap)
+        picked = jnp.where(
+            lax.broadcasted_iota(jnp.int32, factor.shape, 0) == rank, factor, 0.0
+        )
+        amount = jnp.sum(picked[:, 0:1])
+        out_ref[b] = weights_ref[b] - amount * landed[slot].astype(jnp.float32)
+
+    @pl.loop(1, n)
+    def _(k):
+        transfer(k, lax.rem(me + k, n), me).wait_send()
+        tiny(k, lax.rem(me + k, n), me).wait_send()
+
+
+def kernels_fit(rows, width):
+    return lax.axis_size("dp") == 2 and rows % 32 == 0 and width % 128 == 0
+
+
+def fast(
+    grad_parts, weights, left_stat, right_stat, left_codes, right_codes,
+    left_scales, right_scales, owners,
+):
+    n = lax.axis_size("fsdp")
+    replica = lax.axis_index("dp")
+    cap, width, size = left_stat.shape
+    blocks, rows = weights.shape[:2]
+    half = rows // 2
+    slot_of = slot_table(owners, cap)
+    slot_ids = jnp.arange(n * cap, dtype=jnp.int32)
+    matches = slot_of[None, :] == slot_ids[:, None]
+    block_ids = jnp.arange(blocks, dtype=jnp.int32)
+    source = jnp.sum(jnp.where(matches, block_ids[None, :] + 1, 0), axis=1) - 1
+
+    vmem = pl.BlockSpec(memory_space=pltpu.VMEM)
+    smem = pl.BlockSpec(memory_space=pltpu.SMEM)
+    dma = pltpu.SemaphoreType.DMA
+    whole_grad = pl.pallas_call(
+        functools.partial(scatter_kernel, n, cap),
+        out_shape=jax.ShapeDtypeStruct((cap, size, size), jnp.bfloat16),
+        in_specs=[smem, vmem],
+        out_specs=vmem,
+        scratch_shapes=[
+            pltpu.VMEM((blocks, half, size), jnp.bfloat16),
+            pltpu.VMEM((blocks, half, size), jnp.bfloat16),
+            pltpu.VMEM((n * cap, half, size), jnp.bfloat16),
+            dma, dma, dma((n,)), dma((n,)), dma((n,)), dma((n,)), dma,
+        ],
+        compiler_params=pltpu.CompilerParams(collective_id=0, has_side_effects=True),
+    )(source, grad_parts[0])
+
+    left_factor = (left_codes.astype(jnp.float32) * left_scales[:, :, None]).astype(jnp.bfloat16)
+    right_factor = (right_codes.astype(jnp.float32) * right_scales[:, :, None]).astype(jnp.bfloat16)
+    mixed = jnp.einsum(
+        "sik,sck->sic", whole_grad, right_factor, preferred_element_type=jnp.float32
+    ).astype(jnp.bfloat16)
+    precond = jnp.einsum("sik,skc->sic", left_factor, mixed, preferred_element_type=jnp.float32)
+    part_squares = jnp.sum(precond * precond, axis=(1, 2))
+    grad_squares = jnp.sum(jnp.square(whole_grad.astype(jnp.float32)), axis=(1, 2))
+    squares = jnp.stack([part_squares, grad_squares])
+    squares = jnp.pad(squares, ((0, 0), (0, (-cap) % 8)))
+    squares = jnp.broadcast_to(squares[:, :, None], squares.shape + (128,))
+
+    lanes = squares.shape[1:]
+    new_weights = pl.pallas_call(
+        functools.partial(return_kernel, n, cap),
+        out_shape=jax.ShapeDtypeStruct(weights.shape, jnp.float32),
+        in_specs=[smem, smem, vmem, vmem, vmem],
+        out_specs=vmem,
+        scratch_shapes=[
+            pltpu.VMEM((n * cap, rows, width), jnp.bfloat16),
+            pltpu.VMEM(squares.shape, jnp.float32),
+            pltpu.VMEM(lanes, jnp.float32),
+            pltpu.VMEM((n,) + lanes, jnp.float32),
+            dma, dma, dma((n,)), dma((n,)), dma((n,)), dma((n,)),
+        ],
+        compiler_params=pltpu.CompilerParams(collective_id=1, has_side_effects=True),
+    )(slot_of, owners, precond.astype(jnp.bfloat16), squares, weights)
+
+    first_row = replica * width
+    rows_mine = lax.dynamic_slice_in_dim(whole_grad, first_row, width, 1)
+    cols_mine = lax.dynamic_slice_in_dim(whole_grad, first_row, width, 2)
+    gram_left = jnp.einsum("srk,sck->src", rows_mine, whole_grad, preferred_element_type=jnp.float32)
+    gram_right = jnp.einsum("skr,skc->src", cols_mine, whole_grad, preferred_element_type=jnp.float32)
+    left_new = stat_decay * left_stat + (1.0 - stat_decay) * gram_left
+    right_new = stat_decay * right_stat + (1.0 - stat_decay) * gram_right
+    return (new_weights, left_new, right_new)
+
+
 def route_rows(summed, picker, owner_count, capacity):
     blocks = summed.shape[0]
     flat = summed.reshape(blocks, -1)
@@ -26,16 +271,14 @@
 
 
 def local(
-    grad_parts,
-    weights,
-    left_stat,
-    right_stat,
-    left_codes,
-    right_codes,
-    left_scales,
-    right_scales,
-    owners,
+    grad_parts, weights, left_stat, right_stat, left_codes, right_codes,
+    left_scales, right_scales, owners,
 ):
+    if kernels_fit(weights.shape[1], left_stat.shape[1]):
+        return fast(
+            grad_parts, weights, left_stat, right_stat, left_codes, right_codes,
+            left_scales, right_scales, owners,
+        )
     owner_count = lax.axis_size("fsdp")
     replica = lax.axis_index("dp")
     capacity = left_stat.shape[0]

time: 134 us -> 73.7 us (0.55)
  the two profiles are of different devices: /device:TPU:16 before, /device:TPU:0 now
where the time goes in v1:
time: 73.7 us; the launch traced here: 73.5 us
  Pallas kernels  60.3 us (82%)
  matrix products  6.74 us (9%)
  other arithmetic  4.21 us (6%)
  local copies, waits for them, and re-layouts  1.5 us (2%)
    pallas_call x1, Pallas kernels, fast(): pl.pallas_call(functools.partial(return_kernel, n, cap), out_shape=jax.Sh...  35.1 us
    pallas_call x1, Pallas kernels, fast(): pl.pallas_call(functools.partial(scatter_kernel, n, cap), out_shape=jax.S...  25.2 us
    dot_general x1, matrix products, fast(): jnp.einsum('sik,skc->sic', left_factor, mixed, preferred_element_type=jnp...  3.15 us
    reduce_sum x1, other arithmetic, fast(): jnp.sum(jnp.square(whole_grad.astype(jnp.float32)), axis=(1, 2))  2.02 us
    dot_general x1, matrix products, fast(): jnp.einsum('skr,skc->src', cols_mine, whole_grad, preferred_element_type=...  1.81 us
    dot_general x1, matrix products, fast(): jnp.einsum('srk,sck->src', rows_mine, whole_grad, preferred_element_type=...  1.79 us

profile of v1, /device:TPU:0, one launch (start us, length us, event | category | flops | bytes accessed | tf_op | source)
XLA Modules:
  0.0 73.5 jit_solution(14878927382603388817)
XLA Ops:
  0.6 0.9 %convert_reduce_fusion = s32[16]{0:T(128)S(1)} fusion(s32[16]{0:T(128)} %scale_row_ref.1), kind=kLoop, calls=%fused_computation.14 | loop fusion | flops 1264 | bytes 128 | tf_op jit(solution)/shard_map/reduce_sum | solution.py:20
  1.5 0.7 iota_add_fusion
  2.2 0.0 copy-start.4
  2.2 0.1 select_reduce_fusion
  2.3 0.5 broadcast_add_fusion.source_ref
  2.8 0.0 copy-start.5
  2.8 0.0 copy-start.6
  2.8 0.0 copy-start.7
  2.8 25.2 %shard_map.112 = bf16[3,512,512]{2,1,0:T(8,128)(2,1)} custom-call(s32[48]{0:T(128)} %broadcast_add_fusion.source_ref, bf16[16,32,512]{2,1,0:T(8,128)(2,1)} %bitcast.6), custom_call_target="tpu_custom_call" | custom-call | tf_op jit(solution)/shard_map/pallas_call | solution.py:212
  28.1 0.0 copy-start
  28.1 2.0 %multiply_reduce_fusion = f32[3]{0:T(128)S(1)} fusion(bf16[3,512,512]{2,1,0:T(8,128)(2,1)} %shard_map.112), kind=kLoop, calls=%fused_computation | loop fusion | flops 2359293 | bytes 1572876 | tf_op jit(solution)/shard_map/reduce_sum | solution.py:233
  30.1 0.0 copy-done.4
  30.1 0.0 copy-done.5
  30.1 0.0 copy-done.6
  30.1 0.0 copy-done.7
  30.1 0.0 copy-done
  30.1 3.2 %multiply_reduce_fusion.1 = (f32[3]{0:T(128)S(1)}, bf16[3,512,256]{2,1,0:T(8,128)(2,1)}) fusion(bf16[3,512,512]{2,1,0:T(8,128)(2,1)S(1)} %copy-done, bf16[3,256,512]{2,1,0:T(8,128)(2,1)} %param.14, f32[3,256]{1,0:T(4,128)S(1)} %copy-done.7, bf16[3,512,512]{2,1,0:T(8,128)(2,1)S(1)} %copy-done.5, f32[3,512]{1,0:T(4,128)S(1)} %copy-done.6), kind=kOutput, calls=%fused_computation.5 | convolution fusion | flops 810418176 | bytes 4727820 | tf_op jit(solution)/shard_map/sik,skc->sic/dot_general | solution.py:231
  33.3 0.0 copy-start.2
  33.3 0.7 broadcast_in_dim.16.squares_ref
  34.0 35.1 %shard_map.113 = f32[16,32,256]{2,1,0:T(8,128)} custom-call(s32[16]{0:T(128)} %copy-done.4, s32[16]{0:T(128)} %scale_row_ref.1, bf16[3,512,256]{2,1,0:T(8,128)(2,1)} %get-tuple-element.4.pre_ref, f32[2,8,128]{2,1,0:T(8,128)} %broadcast_in_dim.16.squares_ref, f32[16,32,256]{2,1,0:T(8,128)} %weights_ref.1), custom_call_target="tpu_custom_call" | custom-call | tf_op jit(solution)/shard_map/pallas_call | solution.py:239
  69.1 0.0 copy-done.2
  69.1 0.0 copy-start.3
  69.1 1.8 %multiply_add_fusion.1 = f32[3,256,512]{2,1,0:T(8,128)} fusion(f32[3,256,512]{2,1,0:T(8,128)S(1)} %copy-done.2, bf16[3,512,512]{2,1,0:T(8,128)(2,1)S(1)} %copy-done, s32[]{:T(128)S(6)} %select_n.9), kind=kOutput, calls=%fused_computation.4 | convolution fusion | flops 403832832 | bytes 5505028 | tf_op jit(solution)/shard_map/srk,sck->src/dot_general | solution.py:257
  70.9 0.0 copy-done.3
  70.9 0.0 copy-start.1
  70.9 1.8 %multiply_add_fusion = f32[3,256,512]{2,1,0:T(8,128)} fusion(f32[3,256,512]{2,1,0:T(8,128)S(1)} %copy-done.3, bf16[3,512,512]{2,1,0:T(8,128)(2,1)S(1)} %copy-done, s32[]{:T(128)S(6)} %select_n.9), kind=kOutput, calls=%fused_computation.3 | convolution fusion | flops 403832832 | bytes 5505028 | tf_op jit(solution)/shard_map/skr,skc->src/dot_general | solution.py:258
  72.7 0.0 copy-done.1
  72.7 0.8 %copy.16 = f32[16,32,256]{2,1,0:T(8,128)} copy(f32[16,32,256]{2,1,0:T(8,128)S(1)} %copy-done.1) | data formatting | bytes 1048576
  (1 shorter events, 0.0 us)
Async XLA Ops:
  2.2 27.9 %copy-start.4 = (s32[16]{0:T(128)}, s32[16]{0:T(128)S(1)}, u32[]{:S(2)}) copy-start(s32[16]{0:T(128)S(1)} %get-tuple-element.7.place_ref) | copy-start | bytes 196
  2.8 27.3 %copy-start.5 = (bf16[3,512,512]{2,1,0:T(8,128)(2,1)S(1)}, bf16[3,512,512]{2,1,0:T(8,128)(2,1)}, u32[]{:S(2)}) copy-start(bf16[3,512,512]{2,1,0:T(8,128)(2,1)} %param.13) | copy-start | bytes 4718596
  2.8 27.3 %copy-start.6 = (f32[3,512]{1,0:T(4,128)S(1)}, f32[3,512]{1,0:T(4,128)}, u32[]{:S(2)}) copy-start(f32[3,512]{1,0:T(4,128)} %param.15) | copy-start | bytes 18436
  2.8 27.3 %copy-start.7 = (f32[3,256]{1,0:T(4,128)S(1)}, f32[3,256]{1,0:T(4,128)}, u32[]{:S(2)}) copy-start(f32[3,256]{1,0:T(4,128)} %param.16) | copy-start | bytes 9220
  28.1 2.0 %copy-start = (bf16[3,512,512]{2,1,0:T(8,128)(2,1)S(1)}, bf16[3,512,512]{2,1,0:T(8,128)(2,1)}, u32[]{:S(2)}) copy-start(bf16[3,512,512]{2,1,0:T(8,128)(2,1)} %shard_map.112) | copy-start | bytes 4718596
  33.3 35.8 %copy-start.2 = (f32[3,256,512]{2,1,0:T(8,128)S(1)}, f32[3,256,512]{2,1,0:T(8,128)}, u32[]{:S(2)}) copy-start(f32[3,256,512]{2,1,0:T(8,128)} %param.11) | copy-start | bytes 4718596
  69.1 1.8 %copy-start.3 = (f32[3,256,512]{2,1,0:T(8,128)S(1)}, f32[3,256,512]{2,1,0:T(8,128)}, u32[]{:S(2)}) copy-start(f32[3,256,512]{2,1,0:T(8,128)} %param.12) | copy-start | bytes 4718596
  70.9 1.8 %copy-start.1 = (f32[16,32,256]{2,1,0:T(8,128)S(1)}, f32[16,32,256]{2,1,0:T(8,128)}, u32[]{:S(2)}) copy-start(f32[16,32,256]{2,1,0:T(8,128)} %shard_map.113) | copy-start | bytes 1572868

commit v2 on v0

--- a/solution.py
+++ b/solution.py
@@ -1,11 +1,16 @@
+import functools
+
 import jax
 import jax.numpy as jnp
 from jax import lax
+from jax.experimental import pallas as pl
+from jax.experimental.pallas import tpu as pltpu
 from jax.sharding import PartitionSpec as P
 
 stat_decay = 0.95
 step_size = 0.5
 epsilon = 1e-06
+MESH = pl.DeviceIdType.MESH
 
 
 def slot_table(owners, capacity):
@@ -16,6 +21,280 @@
     return owners * capacity + rank
 
 
+def greet(n, me, core):
+    barrier = pltpu.get_barrier_semaphore()
+
+    @pl.loop(1, n)
+    def _(k):
+        peer = lax.rem(me + k, n)
+        pl.semaphore_signal(barrier, inc=1, device_id=(peer, core), device_id_type=MESH)
+
+    pl.semaphore_signal(barrier, inc=1, device_id=(me, 1 - core), device_id_type=MESH)
+    pl.semaphore_wait(barrier, n)
+
+
+def step_kernel(
+    n, cap, source_ref, slot_ref, owner_ref, rank_ref,
+    grad_ref, left_scale_ref, right_scale_ref, left_hbm, right_hbm, weights_hbm,
+    whole, out_ref,
+    theirs, summed, stage, left_ref, right_ref, weights_ref, mixed_ref, pre_ref, landed,
+    squares, other_squares, graft, grafts,
+    load_sem, swap_send, swap_recv, own_sem, out_send, out_recv, fwd_send, fwd_recv,
+    back_send, back_recv, sq_send, sq_recv, tiny_send, tiny_recv,
+):
+    me = lax.axis_index("fsdp")
+    core = lax.axis_index("dp")
+    blocks, rows, size = grad_ref.shape
+    half = rows // 2
+    loads = [
+        pltpu.make_async_copy(right_hbm, right_ref, load_sem.at[0]),
+        pltpu.make_async_copy(left_hbm, left_ref, load_sem.at[1]),
+        pltpu.make_async_copy(weights_hbm, weights_ref, load_sem.at[2]),
+    ]
+    for load in loads:
+        load.start()
+    greet(n, me, core)
+
+    other_rows = pl.ds(pl.multiple_of((1 - core) * half, half), half)
+    my_rows = pl.ds(pl.multiple_of(core * half, half), half)
+    swap = pltpu.make_async_remote_copy(
+        src_ref=grad_ref.at[:, other_rows, :], dst_ref=theirs,
+        send_sem=swap_send, recv_sem=swap_recv,
+        device_id=(me, 1 - core), device_id_type=MESH,
+    )
+    swap.start()
+    swap.wait()
+    summed[...] = (
+        grad_ref[:, my_rows, :].astype(jnp.float32) + theirs[...].astype(jnp.float32)
+    ).astype(jnp.bfloat16)
+
+    def landing(slot, device, its_core):
+        start = pl.multiple_of(device * rows + its_core * half, half)
+        return whole.at[slot, pl.ds(start, half), :]
+
+    def outward(slot, k, peer, origin):
+        return pltpu.make_async_remote_copy(
+            src_ref=stage.at[slot, peer], dst_ref=landing(slot, origin, core),
+            send_sem=out_send.at[slot, k], recv_sem=out_recv.at[slot, k],
+            device_id=(peer, core), device_id_type=MESH,
+        )
+
+    def forward(slot, k, its_core):
+        peer = lax.rem(me - k + n, n)
+        return pltpu.make_async_remote_copy(
+            src_ref=landing(slot, peer, its_core), dst_ref=landing(slot, peer, its_core),
+            send_sem=fwd_send.at[slot, k], recv_sem=fwd_recv.at[slot, k],
+            device_id=(me, 1 - core), device_id_type=MESH,
+        )
+
+    def back(slot, k, peer, origin):
+        return pltpu.make_async_remote_copy(
+            src_ref=pre_ref.at[slot, pl.ds(pl.multiple_of(peer * rows, rows), rows), :],
+            dst_ref=landed.at[origin * cap + slot],
+            send_sem=back_send.at[slot, k], recv_sem=back_recv.at[slot, k],
+            device_id=(peer, core), device_id_type=MESH,
+        )
+
+    def tiny(k, peer, origin):
+        return pltpu.make_async_remote_copy(
+            src_ref=graft, dst_ref=grafts.at[origin],
+            send_sem=tiny_send.at[k], recv_sem=tiny_recv.at[k],
+            device_id=(peer, core), device_id_type=MESH,
+        )
+
+    def swap_squares(slot):
+        return pltpu.make_async_remote_copy(
+            src_ref=squares.at[slot], dst_ref=other_squares.at[slot],
+            send_sem=sq_send.at[slot], recv_sem=sq_recv.at[slot],
+            device_id=(me, 1 - core), device_id_type=MESH,
+        )
+
+    def own(slot):
+        return pltpu.make_async_copy(stage.at[slot, me], landing(slot, me, core), own_sem.at[slot])
+
+    far = n // 2 - 2
+
+    def nth(i):
+        return 1 + lax.rem(i + far, n - 1)
+
+    @pl.loop(0, cap)
+    def _(slot):
+        @pl.loop(0, n)
+        def _(peer):
+            code = source_ref[peer * cap + slot]
+            piece = summed[lax.max(code, 0)].astype(jnp.float32)
+            keep = jnp.where(code >= 0, 1.0, 0.0).astype(jnp.float32)
+            stage[slot, peer] = (piece * keep).astype(jnp.bfloat16)
+
+        own(slot).start()
+
+        @pl.loop(0, n - 1)
+        def _(i):
+            k = nth(i)
+            outward(slot, k, lax.rem(me + k, n), me).start()
+
+    @pl.loop(0, cap)
+    def _(slot):
+        own(slot).wait()
+        forward(slot, 0, core).start()
+
+    for load in loads:
+        load.wait()
+
+    def scaled(codes, scale_row):
+        count = codes.shape[0]
+        column = jnp.transpose(jnp.broadcast_to(scale_row, (8, count)))[:, 0:1]
+        return (codes.astype(jnp.float32) * column).astype(jnp.bfloat16)
+
+    for slot in range(cap):
+        right_ref[slot] = scaled(right_ref[slot], right_scale_ref[pl.ds(slot, 1), :])
+        left_ref[slot] = scaled(left_ref[slot], left_scale_ref[pl.ds(slot, 1), :])
+
+    @pl.loop(0, cap)
+    def _(slot):
+        @pl.loop(0, n - 1)
+        def _(i):
+            k = nth(i)
+            outward(slot, k, me, lax.rem(me - k + n, n)).wait_recv()
+            forward(slot, k, core).start()
+
+        @pl.loop(0, n)
+        def _(k):
+            forward(slot, k, 1 - core).wait_recv()
+
+        mixed_ref[...] = lax.dot_general(
+            whole[slot], right_ref[slot], (((1,), (1,)), ((), ())),
+            preferred_element_type=jnp.float32,
+        ).astype(jnp.bfloat16)
+        pre = jnp.dot(left_ref[slot], mixed_ref[...], preferred_element_type=jnp.float32)
+        pre_ref[slot] = pre.astype(jnp.bfloat16)
+        squares[slot] = jnp.full(squares.shape[1:], jnp.sum(pre * pre), jnp.float32)
+
+        @pl.loop(0, n - 1)
+        def _(i):
+            k = nth(i)
+            back(slot, k, lax.rem(me + k, n), me).start()
+
+        swap_squares(slot).start()
+        landed[me * cap + slot] = pre_ref[slot, pl.ds(pl.multiple_of(me * rows, rows), rows), :]
+
+    line = lax.broadcasted_iota(jnp.int32, graft.shape, 0)
+    factor = jnp.zeros(graft.shape, jnp.float32)
+    for slot in range(cap):
+        energy = jnp.sum(jnp.square(whole[slot].astype(jnp.float32)))
+        swap_squares(slot).wait()
+        total = squares[slot] + other_squares[slot]
+        ratio = step_size * jnp.sqrt(jnp.full(graft.shape, energy, jnp.float32))
+        factor = jnp.where(line == slot, ratio * lax.rsqrt(total + epsilon), factor)
+    graft[...] = factor
+    grafts[me] = factor
+
+    @pl.loop(0, n - 1)
+    def _(i):
+        k = nth(i)
+        tiny(k, lax.rem(me + k, n), me).start()
+
+    @pl.loop(0, cap)
+    def _(slot):
+        @pl.loop(1, n)
+        def _(k):
+            back(slot, k, me, lax.rem(me - k + n, n)).wait_recv()
+
+    @pl.loop(1, n)
+    def _(k):
+        tiny(k, me, lax.rem(me - k + n, n)).wait_recv()
+
+    @pl.loop(0, blocks)
+    def _(b):
+        amount = grafts[owner_ref[b], pl.ds(rank_ref[b], 1), :]
+        update = landed[slot_ref[b]].astype(jnp.float32)
+        for start in range(0, update.shape[1], 128):
+            part = slice(start, start + 128)
+            out_ref[b, :, part] = weights_ref[b, :, part] - amount * update[:, part]
+
+    @pl.loop(0, cap)
+    def _(slot):
+        @pl.loop(1, n)
+        def _(k):
+            peer = lax.rem(me + k, n)
+            outward(slot, k, peer, me).wait_send()
+            back(slot, k, peer, me).wait_send()
+
+        @pl.loop(0, n)
+        def _(k):
+            forward(slot, k, core).wait_send()
+
+    @pl.loop(1, n)
+    def _(k):
+        tiny(k, lax.rem(me + k, n), me).wait_send()
+
+
+def kernels_fit(rows, width, capacity):
+    return lax.axis_size("dp") == 2 and rows % 32 == 0 and width % 128 == 0 and capacity <= 8
+
+
+def fast(
+    grad_parts, weights, left_stat, right_stat, left_codes, right_codes,
+    left_scales, right_scales, owners,
+):
+    n = lax.axis_size("fsdp")
+    replica = lax.axis_index("dp")
+    cap, width, size = left_stat.shape
+    blocks, rows = weights.shape[:2]
+    half = rows // 2
+    slot_of = slot_table(owners, cap)
+    slot_ids = jnp.arange(n * cap, dtype=jnp.int32)
+    matches = slot_of[None, :] == slot_ids[:, None]
+    block_ids = jnp.arange(blocks, dtype=jnp.int32)
+    source = jnp.sum(jnp.where(matches, block_ids[None, :] + 1, 0), axis=1) - 1
+
+    vmem = pl.BlockSpec(memory_space=pltpu.VMEM)
+    smem = pl.BlockSpec(memory_space=pltpu.SMEM)
+    hbm = pl.BlockSpec(memory_space=pl.ANY)
+    dma = pltpu.SemaphoreType.DMA
+    bf16, f32 = jnp.bfloat16, jnp.float32
+    whole_grad, new_weights = pl.pallas_call(
+        functools.partial(step_kernel, n, cap),
+        out_shape=(
+            jax.ShapeDtypeStruct((cap, size, size), bf16),
+            jax.ShapeDtypeStruct(weights.shape, f32),
+        ),
+        in_specs=[smem] * 4 + [vmem] * 3 + [hbm] * 3,
+        out_specs=(vmem, vmem),
+        scratch_shapes=[
+            pltpu.VMEM((blocks, half, size), bf16),
+            pltpu.VMEM((blocks, half, size), bf16),
+            pltpu.VMEM((cap, n, half, size), bf16),
+            pltpu.VMEM(left_codes.shape, bf16),
+            pltpu.VMEM(right_codes.shape, bf16),
+            pltpu.VMEM(weights.shape, f32),
+            pltpu.VMEM((size, width), bf16),
+            pltpu.VMEM((cap, size, width), bf16),
+            pltpu.VMEM((n * cap, rows, width), bf16),
+            pltpu.VMEM((cap, 8, 128), f32),
+            pltpu.VMEM((cap, 8, 128), f32),
+            pltpu.VMEM((8, 128), f32),
+            pltpu.VMEM((n, 8, 128), f32),
+            dma((3,)), dma, dma, dma((cap,)),
+            dma((cap, n)), dma((cap, n)), dma((cap, n)), dma((cap, n)),
+            dma((cap, n)), dma((cap, n)), dma((cap,)), dma((cap,)), dma((n,)), dma((n,)),
+        ],
+        compiler_params=pltpu.CompilerParams(collective_id=0, has_side_effects=True),
+    )(
+        source, slot_of, owners, slot_of - owners * cap,
+        grad_parts[0], left_scales, right_scales, left_codes, right_codes, weights,
+    )
+
+    first_row = replica * width
+    rows_mine = lax.dynamic_slice_in_dim(whole_grad, first_row, width, 1)
+    cols_mine = lax.dynamic_slice_in_dim(whole_grad, first_row, width, 2)
+    gram_left = jnp.einsum("srk,sck->src", rows_mine, whole_grad, preferred_element_type=jnp.float32)
+    gram_right = jnp.einsum("skr,skc->src", cols_mine, whole_grad, preferred_element_type=jnp.float32)
+    left_new = stat_decay * left_stat + (1.0 - stat_decay) * gram_left
+    right_new = stat_decay * right_stat + (1.0 - stat_decay) * gram_right
+    return (new_weights, left_new, right_new)
+
+
 def route_rows(summed, picker, owner_count, capacity):
     blocks = summed.shape[0]
     flat = summed.reshape(blocks, -1)
@@ -26,16 +305,14 @@
 
 
 def local(
-    grad_parts,
-    weights,
-    left_stat,
-    right_stat,
-    left_codes,
-    right_codes,
-    left_scales,
-    right_scales,
-    owners,
+    grad_parts, weights, left_stat, right_stat, left_codes, right_codes,
+    left_scales, right_scales, owners,
 ):
+    if kernels_fit(weights.shape[1], left_stat.shape[1], left_stat.shape[0]):
+        return fast(
+            grad_parts, weights, left_stat, right_stat, left_codes, right_codes,
+            left_scales, right_scales, owners,
+        )
     owner_count = lax.axis_size("fsdp")
     replica = lax.axis_index("dp")
     capacity = left_stat.shape[0]

time: 134 us -> 61.5 us (0.46)
  the two profiles are of different devices: /device:TPU:16 before, /device:TPU:0 now
where the time goes in v2:
time: 61.5 us; the launch traced here: 61.3 us
  Pallas kernels  52.2 us (85%)
  matrix products  5.4 us (9%)
  other arithmetic  2.18 us (4%)
  local copies, waits for them, and re-layouts  0.82 us (1%)
  between operations  0.68 us (1%)
    pallas_call x1, Pallas kernels, fast(): pl.pallas_call(functools.partial(step_kernel, n, cap), out_shape=(jax.Sha...  52.2 us
    dot_general x1, matrix products, fast(): jnp.einsum('srk,sck->src', rows_mine, whole_grad, preferred_element_type=...  3.58 us
    dot_general x1, matrix products, fast(): jnp.einsum('skr,skc->src', cols_mine, whole_grad, preferred_element_type=...  1.81 us

profile of v2, /device:TPU:0, one launch (start us, length us, event | category | flops | bytes accessed | tf_op | source)
XLA Modules:
  0.0 61.3 jit_solution(11207688271877538730)
XLA Ops:
  0.6 0.9 %convert_reduce_fusion.rank_ref = s32[16]{0:T(128)S(1)} fusion(s32[16]{0:T(128)} %owner_ref.1), kind=kLoop, calls=%fused_computation.6 | loop fusion | flops 1264 | bytes 128 | tf_op jit(solution)/shard_map/reduce_sum | solution.py:20
  1.5 0.0 copy-start.4
  1.6 0.7 %iota_add_fusion = (s32[16]{0:T(128)S(1)}, s32[16]{0:T(128)S(1)}) fusion(s32[16]{0:T(128)S(1)} %convert_reduce_fusion.rank_ref, s32[16]{0:T(128)} %owner_ref.1), kind=kLoop, calls=%fused_computation.9 | loop fusion | flops 48 | bytes 256 | tf_op jit(solution)/shard_map/add | solution.py:249
  2.2 0.0 copy-start.5
  2.2 0.1 select_reduce_fusion
  2.3 0.5 broadcast_add_fusion.source_ref
  2.8 0.0 copy-done.4
  2.8 0.0 copy-done.5
  2.8 0.0 copy-start.1
  2.8 52.2 %shard_map.112 = (bf16[3,512,512]{2,1,0:T(8,128)(2,1)}, f32[16,32,256]{2,1,0:T(8,128)}) custom-call(s32[48]{0:T(128)} %broadcast_add_fusion.source_ref, s32[16]{0:T(128)} %copy-done.5, s32[16]{0:T(128)} %owner_ref.1, s32[16]{0:T(128)} %copy-done.4, bf16[16,32,512]{2,1,0:T(8,128)(2,1)} %bitcast.3, f32[3,512]{1,0:T(4,128)} %left_scale_ref.1, ...), custom_call_target="tpu_custom_call" | custom-call | tf_op jit(solution)/shard_map/pallas_call | solution.py:256
  55.1 0.0 copy-done.1
  55.1 0.0 copy-start
  55.1 0.0 copy-start.2
  55.1 3.6 %multiply_add_fusion.1 = f32[3,256,512]{2,1,0:T(8,128)} fusion(f32[3,256,512]{2,1,0:T(8,128)S(1)} %copy-done.1, bf16[3,512,512]{2,1,0:T(8,128)(2,1)} %get-tuple-element.6, s32[]{:T(128)S(6)} %select_n.9), kind=kOutput, calls=%fused_computation.1 | convolution fusion | flops 403832832 | bytes 5505028 | tf_op jit(solution)/shard_map/srk,sck->src/dot_general | solution.py:291
  58.7 0.0 copy-done
  58.7 0.0 copy-done.2
  58.7 0.0 copy-start.3
  58.7 1.8 %multiply_add_fusion = f32[3,256,512]{2,1,0:T(8,128)} fusion(f32[3,256,512]{2,1,0:T(8,128)S(1)} %copy-done.2, bf16[3,512,512]{2,1,0:T(8,128)(2,1)S(1)} %copy-done, s32[]{:T(128)S(6)} %select_n.9), kind=kOutput, calls=%fused_computation | convolution fusion | flops 403832832 | bytes 5505028 | tf_op jit(solution)/shard_map/skr,skc->src/dot_general | solution.py:292
  60.5 0.0 copy-done.3
  60.5 0.8 %copy.16 = f32[16,32,256]{2,1,0:T(8,128)} copy(f32[16,32,256]{2,1,0:T(8,128)S(1)} %copy-done.3) | data formatting | bytes 1048576
Async XLA Ops:
  1.5 1.3 %copy-start.4 = (s32[16]{0:T(128)}, s32[16]{0:T(128)S(1)}, u32[]{:S(2)}) copy-start(s32[16]{0:T(128)S(1)} %convert_reduce_fusion.rank_ref) | copy-start | bytes 196
  2.2 0.6 copy-start.5
  2.8 52.2 %copy-start.1 = (f32[3,256,512]{2,1,0:T(8,128)S(1)}, f32[3,256,512]{2,1,0:T(8,128)}, u32[]{:S(2)}) copy-start(f32[3,256,512]{2,1,0:T(8,128)} %param.11) | copy-start | bytes 4718596
  55.1 3.6 %copy-start = (bf16[3,512,512]{2,1,0:T(8,128)(2,1)S(1)}, bf16[3,512,512]{2,1,0:T(8,128)(2,1)}, u32[]{:S(2)}) copy-start(bf16[3,512,512]{2,1,0:T(8,128)(2,1)} %get-tuple-element.6) | copy-start | bytes 4718596
  55.1 3.6 %copy-start.2 = (f32[3,256,512]{2,1,0:T(8,128)S(1)}, f32[3,256,512]{2,1,0:T(8,128)}, u32[]{:S(2)}) copy-start(f32[3,256,512]{2,1,0:T(8,128)} %param.12) | copy-start | bytes 4718596
  58.7 1.8 %copy-start.3 = (f32[16,32,256]{2,1,0:T(8,128)S(1)}, f32[16,32,256]{2,1,0:T(8,128)}, u32[]{:S(2)}) copy-start(f32[16,32,256]{2,1,0:T(8,128)} %get-tuple-element.12) | copy-start | bytes 1572868

commit v3 on v2

--- a/solution.py
+++ b/solution.py
@@ -30,16 +30,34 @@
         pl.semaphore_signal(barrier, inc=1, device_id=(peer, core), device_id_type=MESH)
 
     pl.semaphore_signal(barrier, inc=1, device_id=(me, 1 - core), device_id_type=MESH)
-    pl.semaphore_wait(barrier, n)
+
+
+def fill_tables(n, cap, blocks, owner_ref, slot_ref, rank_ref, source_ref):
+    slots = []
+    for b in range(blocks):
+        rank = jnp.int32(0)
+        for c in range(b):
+            rank = rank + jnp.where(owner_ref[c] == owner_ref[b], 1, 0).astype(jnp.int32)
+        rank = lax.min(rank, jnp.int32(cap - 1))
+        slots.append(owner_ref[b] * cap + rank)
+        slot_ref[b] = slots[b]
+        rank_ref[b] = rank
+
+    @pl.loop(0, n * cap)
+    def _(j):
+        code = jnp.int32(-1)
+        for b in range(blocks):
+            code = jnp.where(slots[b] == j, jnp.int32(b), code)
+        source_ref[j] = code
 
 
 def step_kernel(
-    n, cap, source_ref, slot_ref, owner_ref, rank_ref,
-    grad_ref, left_scale_ref, right_scale_ref, left_hbm, right_hbm, weights_hbm,
-    whole, out_ref,
-    theirs, summed, stage, left_ref, right_ref, weights_ref, mixed_ref, pre_ref, landed,
+    n, cap, owner_ref, grad_ref, left_scale_ref, right_scale_ref,
+    left_hbm, right_hbm, weights_hbm, left_stat_hbm, right_stat_hbm,
+    out_ref, left_new_ref, right_new_ref,
+    slot_ref, rank_ref, source_ref, whole, left_stat_ref, right_stat_ref, theirs, summed, stage, left_ref, right_ref, weights_ref, mixed_ref, pre_ref, landed,
     squares, other_squares, graft, grafts,
-    load_sem, swap_send, swap_recv, own_sem, out_send, out_recv, fwd_send, fwd_recv,
+    load_sem, store_sem, swap_send, swap_recv, own_sem, out_send, out_recv, fwd_send, fwd_recv,
     back_send, back_recv, sq_send, sq_recv, tiny_send, tiny_recv,
 ):
     me = lax.axis_index("fsdp")
@@ -50,10 +68,14 @@
         pltpu.make_async_copy(right_hbm, right_ref, load_sem.at[0]),
         pltpu.make_async_copy(left_hbm, left_ref, load_sem.at[1]),
         pltpu.make_async_copy(weights_hbm, weights_ref, load_sem.at[2]),
+        pltpu.make_async_copy(left_stat_hbm, left_stat_ref, load_sem.at[3]),
+        pltpu.make_async_copy(right_stat_hbm, right_stat_ref, load_sem.at[4]),
     ]
+    greet(n, me, core)
     for load in loads:
         load.start()
-    greet(n, me, core)
+    fill_tables(n, cap, blocks, owner_ref, slot_ref, rank_ref, source_ref)
+    pl.semaphore_wait(pltpu.get_barrier_semaphore(), n)
 
     other_rows = pl.ds(pl.multiple_of((1 - core) * half, half), half)
     my_rows = pl.ds(pl.multiple_of(core * half, half), half)
@@ -112,10 +134,13 @@
     def own(slot):
         return pltpu.make_async_copy(stage.at[slot, me], landing(slot, me, core), own_sem.at[slot])
 
-    far = n // 2 - 2
+    def store(side, slot):
+        kept = (left_stat_ref, right_stat_ref)[side]
+        result = (left_new_ref, right_new_ref)[side]
+        return pltpu.make_async_copy(kept.at[slot], result.at[slot], store_sem.at[side, slot])
 
     def nth(i):
-        return 1 + lax.rem(i + far, n - 1)
+        return i + 1
 
     @pl.loop(0, cap)
     def _(slot):
@@ -138,7 +163,7 @@
         own(slot).wait()
         forward(slot, 0, core).start()
 
-    for load in loads:
+    for load in loads[:2]:
         load.wait()
 
     def scaled(codes, scale_row):
@@ -194,6 +219,26 @@
         k = nth(i)
         tiny(k, lax.rem(me + k, n), me).start()
 
+    for load in loads[2:]:
+        load.wait()
+    width = left_stat_ref.shape[1]
+    mine = pl.ds(pl.multiple_of(core * width, width), width)
+
+    @pl.loop(0, cap)
+    def _(slot):
+        gram = lax.dot_general(
+            whole[slot, mine, :], whole[slot], (((1,), (1,)), ((), ())),
+            preferred_element_type=jnp.float32,
+        )
+        left_stat_ref[slot] = stat_decay * left_stat_ref[slot] + (1.0 - stat_decay) * gram
+        store(0, slot).start()
+        gram = lax.dot_general(
+            whole[slot, :, mine], whole[slot], (((0,), (0,)), ((), ())),
+            preferred_element_type=jnp.float32,
+        )
+        right_stat_ref[slot] = stat_decay * right_stat_ref[slot] + (1.0 - stat_decay) * gram
+        store(1, slot).start()
+
     @pl.loop(0, cap)
     def _(slot):
         @pl.loop(1, n)
@@ -224,6 +269,9 @@
         def _(k):
             forward(slot, k, core).wait_send()
 
+        store(0, slot).wait()
+        store(1, slot).wait()
+
     @pl.loop(1, n)
     def _(k):
         tiny(k, lax.rem(me + k, n), me).wait_send()
@@ -238,30 +286,30 @@
     left_scales, right_scales, owners,
 ):
     n = lax.axis_size("fsdp")
-    replica = lax.axis_index("dp")
     cap, width, size = left_stat.shape
     blocks, rows = weights.shape[:2]
     half = rows // 2
-    slot_of = slot_table(owners, cap)
-    slot_ids = jnp.arange(n * cap, dtype=jnp.int32)
-    matches = slot_of[None, :] == slot_ids[:, None]
-    block_ids = jnp.arange(blocks, dtype=jnp.int32)
-    source = jnp.sum(jnp.where(matches, block_ids[None, :] + 1, 0), axis=1) - 1
-
     vmem = pl.BlockSpec(memory_space=pltpu.VMEM)
     smem = pl.BlockSpec(memory_space=pltpu.SMEM)
     hbm = pl.BlockSpec(memory_space=pl.ANY)
     dma = pltpu.SemaphoreType.DMA
     bf16, f32 = jnp.bfloat16, jnp.float32
-    whole_grad, new_weights = pl.pallas_call(
+    return pl.pallas_call(
         functools.partial(step_kernel, n, cap),
         out_shape=(
-            jax.ShapeDtypeStruct((cap, size, size), bf16),
             jax.ShapeDtypeStruct(weights.shape, f32),
+            jax.ShapeDtypeStruct(left_stat.shape, f32),
+            jax.ShapeDtypeStruct(right_stat.shape, f32),
         ),
-        in_specs=[smem] * 4 + [vmem] * 3 + [hbm] * 3,
-        out_specs=(vmem, vmem),
+        in_specs=[smem] + [vmem] * 3 + [hbm] * 5,
+        out_specs=(vmem, hbm, hbm),
         scratch_shapes=[
+            pltpu.SMEM((blocks,), jnp.int32),
+            pltpu.SMEM((blocks,), jnp.int32),
+            pltpu.SMEM((n * cap,), jnp.int32),
+            pltpu.VMEM((cap, size, size), bf16),
+            pltpu.VMEM(left_stat.shape, f32),
+            pltpu.VMEM(right_stat.shape, f32),
             pltpu.VMEM((blocks, half, size), bf16),
             pltpu.VMEM((blocks, half, size), bf16),
             pltpu.VMEM((cap, n, half, size), bf16),
@@ -275,24 +323,15 @@
             pltpu.VMEM((cap, 8, 128), f32),
             pltpu.VMEM((8, 128), f32),
             pltpu.VMEM((n, 8, 128), f32),
-            dma((3,)), dma, dma, dma((cap,)),
+            dma((5,)), dma((2, cap)), dma, dma, dma((cap,)),
             dma((cap, n)), dma((cap, n)), dma((cap, n)), dma((cap, n)),
             dma((cap, n)), dma((cap, n)), dma((cap,)), dma((cap,)), dma((n,)), dma((n,)),
         ],
         compiler_params=pltpu.CompilerParams(collective_id=0, has_side_effects=True),
     )(
-        source, slot_of, owners, slot_of - owners * cap,
-        grad_parts[0], left_scales, right_scales, left_codes, right_codes, weights,
-    )
-
-    first_row = replica * width
-    rows_mine = lax.dynamic_slice_in_dim(whole_grad, first_row, width, 1)
-    cols_mine = lax.dynamic_slice_in_dim(whole_grad, first_row, width, 2)
-    gram_left = jnp.einsum("srk,sck->src", rows_mine, whole_grad, preferred_element_type=jnp.float32)
-    gram_right = jnp.einsum("skr,skc->src", cols_mine, whole_grad, preferred_element_type=jnp.float32)
-    left_new = stat_decay * left_stat + (1.0 - stat_decay) * gram_left
-    right_new = stat_decay * right_stat + (1.0 - stat_decay) * gram_right
-    return (new_weights, left_new, right_new)
+        owners, grad_parts[0], left_scales, right_scales,
+        left_codes, right_codes, weights, left_stat, right_stat,
+    )
 
 
 def route_rows(summed, picker, owner_count, capacity):

time: 61.5 us -> 57.9 us (0.941)
  matrix products: 5.4 us -> 0 us
  local copies, waits for them, and re-layouts: 0.82 us -> 5.81 us
  other arithmetic: 2.18 us -> 0 us
  Pallas kernels: 52.2 us -> 51.3 us
    dot_general x2 -> x0, matrix products: 5.4 us -> none  [the longest x1 3.58 us: fast(): jnp.einsum('srk,sck->src', rows_mine, whole_grad, preferred_element_type=...]
    unnamed x13 -> x5, local copies, waits for them, and re-layouts: 0.82 us -> 5.81 us
    reduce_sum x2 -> x0, other arithmetic: 1 us -> none  [the longest x1 0.91 us: slot_table(): rank = jnp.sum(earlier.astype(jnp.int32), axis=1)]
    pallas_call x1, Pallas kernels: 52.2 us -> 51.3 us  [fast(): pl.pallas_call(functools.partial(step_kernel, n, cap), out_shape=(jax.Sha...]
    add x1 -> x0, other arithmetic: 0.66 us -> none  [fast(): source = jnp.sum(jnp.where(matches, block_ids[None, :] + 1, 0), axis=1) - 1]
where the time goes in v3:
time: 57.9 us; the launch traced here: 57.7 us
  Pallas kernels  51.3 us (89%)
  local copies, waits for them, and re-layouts  5.81 us (10%)
  between operations  0.64 us (1%)
    pallas_call x1, Pallas kernels, fast(): pl.pallas_call(functools.partial(step_kernel, n, cap), out_shape=(jax.Sha...  51.3 us
    unnamed x5, local copies, waits for them, and re-layouts  5.81 us

profile of v3, /device:TPU:0, one launch (start us, length us, event | category | flops | bytes accessed | tf_op | source)
XLA Modules:
  0.0 57.7 jit_solution(7663066240890006754)
XLA Ops:
  0.6 51.3 %shard_map.112 = (f32[16,32,256]{2,1,0:T(8,128)}, f32[3,256,512]{2,1,0:T(8,128)}, f32[3,256,512]{2,1,0:T(8,128)}) custom-call(s32[16]{0:T(128)} %owner_ref.1, bf16[16,32,512]{2,1,0:T(8,128)(2,1)} %bitcast.1, f32[3,512]{1,0:T(4,128)} %left_scale_ref.1, f32[3,256]{1,0:T(4,128)} %right_scale_ref.1, bf16[3,512,512]{2,1,0:T(8,128)(2,1)} %left_hbm.1, ...), custom_call_target="tpu_custom_call" | custom-call | tf_op jit(solution)/shard_map/pallas_call | solution.py:297
  51.9 1.9 %copy.15 = f32[16,32,256]{2,1,0:T(8,128)} copy(f32[16,32,256]{2,1,0:T(8,128)} %get-tuple-element.6) | data formatting | bytes 1048576
  53.8 0.0 copy-start
  53.8 2.8 %copy.16 = f32[3,256,512]{2,1,0:T(8,128)} copy(f32[3,256,512]{2,1,0:T(8,128)} %get-tuple-element.7) | data formatting | bytes 3145728
  56.6 0.0 copy-done
  56.6 1.1 %copy.17 = f32[3,256,512]{2,1,0:T(8,128)} copy(f32[3,256,512]{2,1,0:T(8,128)S(1)} %copy-done) | data formatting | bytes 3145728
Async XLA Ops:
  53.8 2.8 %copy-start = (f32[3,256,512]{2,1,0:T(8,128)S(1)}, f32[3,256,512]{2,1,0:T(8,128)}, u32[]{:S(2)}) copy-start(f32[3,256,512]{2,1,0:T(8,128)} %get-tuple-element.8) | copy-start | bytes 4718596
